TPU v7x, 256 devices: a whole 4x4x8 slice. The times are simulated.
256 devices in a mesh: row: 8 (over y, core), col: 32 (over x, z).
Axes of the slice: x: 4, y: 4, z: 8, core: 2. Of those that a mesh axis runs over, the one named last changes fastest.
Arguments:
- features: bfloat16 [65536, 512], P(('row', 'col')), may hold values from -6 to 6
- memory: float32 [65536, 512], P(('col', 'row')), may hold values from -1 to 1
- tile_values: bfloat16 [8, 32, 128, 128, 128], P('row', 'col'), as said below
- tile_rows: int32 [8, 32, 128], P('row', 'col'), may hold values from 0 to 15, as said below
- tile_cols: int32 [8, 32, 128], P('row', 'col'), may hold values from 0 to 63
- tile_count: int32 [8, 32], P('row', 'col'), may hold values from 16 to 128, as said below
- conv_weight: bfloat16 [512, 512], replicated, may hold values from -0.25 to 0.25
- conv_bias: float32 [512], replicated, may hold values from -3 to 3
- input_weight: bfloat16 [512, 1536], replicated, may hold values from -0.25 to 0.25
- input_bias: float32 [1536], replicated, may hold values from -3 to 3
- hidden_weight: bfloat16 [512, 1536], replicated, may hold values from -0.25 to 0.25
- hidden_bias: float32 [1536], replicated, may hold values from -3 to 3
Outputs:
- new_memory: float32 [65536, 512], P(('col', 'row'))
Inputs may be any that keep to these rules, and one draw needn't show every extreme that they name: `tile_values`: edge weights are nonnegative. For each device pair (r, c) the 128 pairs (tile_rows, tile_cols) are distinct. `tile_count`: in every draw some device pair has all 128 slots live.
All inputs are finite; a program needn't handle non-finite values.
Results may differ from a plain program's by a relative error of at most 0.017.
Values may be sent and summed in bfloat16 or wider, within the bound.
A program may use at most 128 MiB of HBM per device.

v0:
```python
import jax
import jax.numpy as jnp
from jax import lax
from jax.sharding import PartitionSpec as P

norm_epsilon = 1e-06
tiles_per_pass = 32


def gru_update(message, memory, input_weight, input_bias, hidden_weight, hidden_bias):
    width = memory.shape[1]
    from_input = jnp.dot(message, input_weight, preferred_element_type=jnp.float32) + input_bias
    held = memory.astype(jnp.bfloat16)
    from_memory = jnp.dot(held, hidden_weight, preferred_element_type=jnp.float32) + hidden_bias
    reset = jax.nn.sigmoid(from_input[:, :width] + from_memory[:, :width])
    update = jax.nn.sigmoid(from_input[:, width : 2 * width] + from_memory[:, width : 2 * width])
    candidate = jnp.tanh(from_input[:, 2 * width :] + reset * from_memory[:, 2 * width :])
    return (1.0 - update) * candidate + update * memory


def on_device(
    features,
    memory,
    tile_values,
    tile_rows,
    tile_cols,
    tile_count,
    conv_weight,
    conv_bias,
    input_weight,
    input_bias,
    hidden_weight,
    hidden_bias,
):
    own_rows, width = features.shape
    tile_data = tile_values[0, 0]
    row_ids = tile_rows[0, 0]
    col_ids = tile_cols[0, 0]
    live_count = tile_count[0, 0]
    slot_total = tile_data.shape[0]
    tile_size = tile_data.shape[1]
    row_blocks = own_rows * lax.axis_size("row") // tile_size
    col_blocks = own_rows * lax.axis_size("col") // tile_size
    per_pass = min(tiles_per_pass, slot_total)
    live = jnp.arange(slot_total) < live_count
    column_sums = jnp.sum(tile_data, axis=1, dtype=jnp.float32) * live[:, None]
    picker = ((col_ids[:, None] == jnp.arange(col_blocks)[None, :]) & live[:, None]).astype(
        jnp.float32
    )
    out_terms = jnp.einsum(
        "tb,tq->bq", picker, column_sums, precision=lax.Precision.HIGHEST
    ).reshape(col_blocks * tile_size)
    gathered = lax.all_gather(features, "col", axis=0, tiled=True)
    all_degree = 1.0 + lax.psum(out_terms.astype(jnp.bfloat16), "col").astype(jnp.float32)
    gathered = (gathered.astype(jnp.float32) * lax.rsqrt(all_degree)[:, None]).astype(jnp.bfloat16)
    panel = gathered.reshape(col_blocks, tile_size, width)

    def advance(block_index, summed):
        first_slot = block_index * per_pass
        block_rows = lax.dynamic_slice_in_dim(row_ids, first_slot, per_pass)
        block_cols = lax.dynamic_slice_in_dim(col_ids, first_slot, per_pass)
        block_tiles = lax.dynamic_slice_in_dim(tile_data, first_slot, per_pass)
        block_live = first_slot + jnp.arange(per_pass) < live_count
        block_tiles = jnp.where(block_live[:, None, None], block_tiles, jnp.zeros((), jnp.bfloat16))
        picked = jnp.take(panel, block_cols, axis=0)
        products = jnp.einsum(
            "tpq,tqf->tpf", block_tiles, picked, preferred_element_type=jnp.float32
        )
        return summed.at[block_rows].add(products)

    passes = (live_count + per_pass - 1) // per_pass
    summed = lax.fori_loop(
        0, passes, advance, jnp.zeros((row_blocks, tile_size, width), jnp.float32)
    )
    partial_value = summed.reshape(row_blocks * tile_size, width)
    owned = lax.psum_scatter(
        partial_value.astype(jnp.bfloat16), "row", scatter_dimension=0, tiled=True
    ).astype(jnp.float32)
    normed = (
        owned / jnp.sqrt(jnp.mean(owned * owned, axis=1, keepdims=True) + norm_epsilon)
    ).astype(jnp.bfloat16)
    message = jax.nn.relu(
        jnp.dot(normed, conv_weight, preferred_element_type=jnp.float32) + conv_bias
    ).astype(jnp.bfloat16)
    return gru_update(message, memory, input_weight, input_bias, hidden_weight, hidden_bias)


def solution(mesh):
    placed = (
        P(("row", "col"), None),
        P(("col", "row"), None),
        P("row", "col", None, None, None),
        P("row", "col", None),
        P("row", "col", None),
        P("row", "col"),
        P(),
        P(),
        P(),
        P(),
        P(),
        P(),
    )
    return jax.shard_map(
        on_device, mesh=mesh, in_specs=placed, out_specs=P(("col", "row"), None), check_vma=False
    )
```

profile of v0, /device:TPU:2, one launch (start us, length us, event | category | flops | bytes accessed | tf_op | source)
XLA Modules:
  0.0 344.4 jit_solution(16640008878866599915)
XLA Ops:
  6.5 0.0 copy-start
  6.5 0.0 all-gather.2.cloned.1.call-start
  6.5 0.7 all-gather.2.cloned.1.call-update
  7.3 0.0 reduce-scatter.2.cloned.1.call-start
  8.0 3.4 convert_reduce_fusion
  11.4 0.0 copy-done.1
  11.4 0.3 fusion.13
  11.7 134.5 %psum.7 = bf16[8192]{0:T(1024)(128)(2,1)S(1)} all-reduce(bf16[8192]{0:T(1024)(128)(2,1)S(1)} %fusion.13), channel_id=1, replica_groups=mesh['row'=8,'col'=32] {'col'}, use_global_device_ids=true, to_apply=%region_1.0 | all-reduce | flops 8192 | bytes 32768 | tf_op jit(solution)/shard_map/psum | solution.py:54
  146.3 0.0 all-gather.2.cloned.1.call-done
  146.3 7.6 %multiply_convert_fusion = bf16[8192,512]{1,0:T(8,128)(2,1)} fusion(bf16[8192,512]{1,0:T(8,128)(2,1)} %all-gather.2.cloned.1.call-done, f32[8192]{0:T(1024)S(1)} %add_rsqrt_fusion), kind=kLoop, calls=%fused_computation.18 | loop fusion | flops 12582912 | bytes 16809984 | tf_op jit(solution)/shard_map/convert_element_type | solution.py:55
  153.9 2.5 broadcast_in_dim.39
  156.4 32.4 %while.10 = (s32[]{:T(128)}, f32[16,128,512]{2,1,0:T(8,128)}, s32[]{:T(128)}, s32[128]{0:T(128)S(1)}, s32[]{:T(128)}, /*index=5*/bf16[128,128,128]{2,1,0:T(8,128...) while((s32[]{:T(128)}, f32[16,128,512]{2,1,0:T(8,128)}, ...), condition=%wide.region_4.5_spmd, body=%wide.region_2.4_spmd.sunk | while | flops 541590912 | bytes 47191224 | solution.py:72
  156.4 0.7 compare_and_fusion.2
  157.2 6.1 %gather_fusion = bf16[32,128,512]{2,1,0:T(8,128)(2,1)} fusion(bf16[64,128,512]{2,1,0:T(8,128)(2,1)} %get-tuple-element.157, s32[1024]{0:T(1024)S(1)} %pad_clamp_fusion.2), kind=kCustom, calls=%fused_computation.clone.1 | custom fusion | bytes 8388736 | tf_op jit(solution)/shard_map/while/body/jit(_take)/gather | solution.py:65
  163.3 7.0 %fusion.51 = f32[32,128,512]{2,1,0:T(8,128)} fusion(bf16[32,128,512]{2,1,0:T(8,128)(2,1)} %gather_fusion, pred[32]{0:T(512)(128)(4,1)S(1)} %get-tuple-element.124, bf16[128,128,128]{2,1,0:T(8,128)(2,1)} %get-tuple-element.155, s32[]{:T(128)S(6)} %select_n.41, pred[32]{0:T(512)(128)(4,1)S(1)} %get-tuple-element.125), kind=kOutput, calls=%fused_computation.2.clone.1 | convolution fusion | flops 539492352 | bytes 13631556 | tf_op jit(solution)/shard_map/while/body/tpq,tqf->tpf/dot_general | solution.py:66
  170.4 0.1 compare_select_fusion.4
  170.4 18.4 %scatter_fusion = f32[16,128,512]{2,1,0:T(8,128)} fusion(f32[16,128,512]{2,1,0:T(8,128)} %get-tuple-element.139, s32[32]{0:T(128)S(1)} %compare_select_fusion.4, f32[32,128,512]{2,1,0:T(8,128)} %fusion.51), kind=kCustom, calls=%fused_computation.1.clone.1 | custom fusion | flops 2097152 | bytes 25165952 | tf_op jit(solution)/shard_map/while/body/scatter-add | solution.py:69
  188.8 3.8 %convert_element_type.52 = bf16[16,128,512]{2,1,0:T(8,128)(2,1)} convert(f32[16,128,512]{2,1,0:T(8,128)} %get-tuple-element.48) | non-fusion elementwise | flops 1048576 | bytes 6291456 | tf_op jit(solution)/shard_map/convert_element_type | solution.py:77
  192.7 0.0 reduce-scatter.2.cloned.1.call-update
  192.7 1.6 convolution_add_fusion
  194.3 135.7 %reduce-scatter.2.cloned.1.call-done = bf16[256,512]{1,0:T(8,128)(2,1)} async-done(((bf16[2048,512]{1,0:T(8,128)(2,1)}), bf16[256,512]{1,0:T(8,128)(2,1)}) %reduce-scatter.2.cloned.1.call-update) | async-done | bytes 262160 | tf_op jit(solution)/shard_map/reduce_scatter | solution.py:76
  330.0 1.1 fusion.14
  331.1 3.7 %convolution_add_fusion.1 = f32[256,1536]{1,0:T(8,128)} fusion(bf16[512,1536]{1,0:T(8,128)(2,1)} %param.22, bf16[512,512]{1,0:T(8,128)(2,1)} %param.20, f32[1536]{0:T(1024)S(1)} %copy-done.3, bf16[256,512]{1,0:T(8,128)(2,1)} %reduce-scatter.2.cloned.1.call-done, f32[512]{0:T(512)S(1)} %copy-done.4, f32[256]{0:T(256)S(1)} %add_sqrt_fusion), kind=kOutput, calls=%fused_computation.21 | convolution fusion | flops 538050560 | bytes 3941376 | tf_op jit(solution)/shard_map/dot_general | solution.py:12
  334.8 2.8 fusion.19
  (14 shorter events, 0.1 us)
Async XLA Ops:
  6.5 186.1 %copy-start = (bf16[512,1536]{1,0:T(8,128)(2,1)S(1)}, bf16[512,1536]{1,0:T(8,128)(2,1)}, u32[]{:S(2)}) copy-start(bf16[512,1536]{1,0:T(8,128)(2,1)} %param.24) | copy-start | bytes 4718596
  6.5 4.9 %copy-start.1 = (s32[1,1,128]{2,1,0:T(1,128)S(1)}, s32[1,1,128]{2,1,0:T(1,128)}, u32[]{:S(2)}) copy-start(s32[1,1,128]{2,1,0:T(1,128)} %param.18) | copy-start | bytes 1540
  6.5 139.8 %all-gather.2.cloned.1.call-start = ((), (), s32[]{:S(2)}) async-start(), calls=%async_computation.1 | async-start | bytes 8650752 | tf_op jit(solution)/shard_map/all_gather | solution.py:53
  7.3 322.8 %reduce-scatter.2.cloned.1.call-start = ((), (), s32[]{:S(2)}) async-start(), calls=%async_computation.2 | async-start | bytes 2359296 | tf_op jit(solution)/shard_map/reduce_scatter | solution.py:76
  153.9 2.5 copy-start.5
  188.8 3.9 %copy-start.2 = (f32[1536]{0:T(1024)S(1)}, f32[1536]{0:T(1024)}, u32[]{:S(2)}) copy-start(f32[1536]{0:T(1024)} %param.25) | copy-start | bytes 18436
  192.6 138.5 %copy-start.3 = (f32[1536]{0:T(1024)S(1)}, f32[1536]{0:T(1024)}, u32[]{:S(2)}) copy-start(f32[1536]{0:T(1024)} %param.23) | copy-start | bytes 18436
  192.7 138.5 %copy-start.4 = (f32[512]{0:T(512)S(1)}, f32[512]{0:T(512)}, u32[]{:S(2)}) copy-start(f32[512]{0:T(512)} %param.21) | copy-start | bytes 6148
Sparse Core Ops, SparseCore 0:
  10.0 101.1 all-gather.1
  192.8 137.1 reduce-scatter.1
where the time goes:
time: 345 us; the launch traced here: 344 us
  waiting for transfers between devices  136 us (39%)
  blocking collectives  135 us (39%)
  other arithmetic  37.9 us (11%)
  between operations  14.2 us (4%)
  matrix products  12.6 us (4%)
  local copies, waits for them, and re-layouts  8.65 us (3%)
    reduce_scatter x1, waiting for transfers between devices, on_device(): lax.psum_scatter(partial_value.astype(jnp.bfloat16), 'row', scatter_dimen...  136 us
    psum x1, blocking collectives, on_device(): lax.psum(out_terms.astype(jnp.bfloat16), 'col').astype(jnp.float32)  135 us
    scatter-add x1, other arithmetic, advance(): return summed.at[block_rows].add(products)  18.4 us
    convert_element_type x1, other arithmetic, on_device(): (gathered.astype(jnp.float32) * lax.rsqrt(all_degree)[:, None]).astype(jn...  7.63 us
    dot_general x1, matrix products, advance(): jnp.einsum('tpq,tqf->tpf', block_tiles, picked, preferred_element_type=jn...  7.04 us
  transfers between devices with their start and end apart: 2, of which 1 were waited for; matrix products, arithmetic and copies ran while one was open for 2% of the time, Pallas kernels for 0%

commit v1 on v0

v1 whole, which is shorter than its diff:
```python
import functools

import jax
import jax.numpy as jnp
from jax import lax
from jax.experimental import pallas as pl
from jax.experimental.pallas import tpu as pltpu
from jax.sharding import PartitionSpec as P

norm_epsilon = 1e-06
NX, NZ = 4, 8
NY = 4
ROWS_A = 96
N_CHUNK = 2
GROUP = 2
MESH = pl.DeviceIdType.MESH
F32 = jnp.float32
BF16 = jnp.bfloat16


def block_units(f, part, rows):
    lo, hi = rows
    mid = (lo + hi) // 2
    units, at = {}, {(0, 0): []}
    n1, n2 = (NX, NZ) if part == 0 else (NZ, NX)
    first, second = ("x", "z") if part == 0 else ("z", "x")

    def offset(d1, d2):
        return (d1, d2) if part == 0 else (d2, d1)

    def ring(axis, n, place):
        for d in range(1, n // 2):
            for sign in (1, -1):
                key = (f, part, *place(sign * d), 2)
                units[key] = (axis, sign, lo, hi, list(at[place(sign * (d - 1))]))
                at[place(sign * d)] = [key]
        far = place(n // 2)
        at[far] = []
        for half, (sign, a, b) in enumerate(((1, lo, mid), (-1, mid, hi))):
            key = (f, part, *far, half)
            units[key] = (axis, sign, a, b, list(at[place(sign * (n // 2 - 1))]))
            at[far].append(key)

    ring(first, n1, lambda d: offset(d, 0))
    for d1 in [0] + [s * d for d in range(1, n1 // 2) for s in (1, -1)] + [n1 // 2]:
        ring(second, n2, lambda d, d1=d1: offset(d1, d))
    return units, at


def make_plan(block_rows, width):
    units, arrivals = {}, {}
    for f in range(N_CHUNK):
        for part, rows in ((0, (0, ROWS_A)), (1, (ROWS_A, block_rows))):
            more, at = block_units(f, part, rows)
            units.update(more)
            for place, keys in at.items():
                arrivals.setdefault((f, *place), []).extend(keys)
    per_row = width // N_CHUNK * 2 * 2 / 90e3
    hop = 0.9
    length = {k: (u[3] - u[2]) * per_row for k, u in units.items()}
    after = {k: [] for k in units}
    for k, u in units.items():
        for p in u[4]:
            after[p].append(k)
    tail = {}

    def tail_of(k):
        if k not in tail:
            tail[k] = length[k] + hop + max([tail_of(j) for j in after[k]], default=0.0)
        return tail[k]

    order = sorted(units, key=lambda k: (k[0], -tail_of(k), k))
    lanes = [(a, s) for a in "xz" for s in (1, -1)]
    arrived, free, busy = {}, dict.fromkeys(lanes, 0.0), {lane: [] for lane in lanes}
    left = list(order)
    cost = 16.5 / (N_CHUNK * 16) * GROUP / 2
    tasks = [
        ["sums", 0, None, 2.0, 1.0],
        ["sums", 1, "sums0", 0.0, 1.0],
        ["degrees", 0, "sums1", 0.0, 1.5],
        ["degrees", 1, "degrees0", 5.0, 1.5],
        ["scale", 0, "degrees1", 4.0, 1.0],
        ["scale", 1, "scale0", 0.0, 1.0],
    ]
    for f in range(N_CHUNK):
        tasks += [
            ["reduce", 4 * f, f"all{f}", 0.0, 0.5],
            ["reduce", 4 * f + 1, f"reduce{4 * f}", 3.5, 0.5],
            ["reduce", 4 * f + 2, f"reduce{4 * f + 1}", 5.0, 0.3],
            ["reduce", 4 * f + 3, f"reduce{4 * f + 2}", 5.0, 0.3],
        ]
    tasks.append(["held", 0, "scale1", 0.0, 2.0])
    sources = [p for p in arrivals if p not in [(f, 0, 0) for f in range(N_CHUNK)]]
    waiting = [(f, 0, 0) for f in range(N_CHUNK)] + sources
    count = dict.fromkeys(range(N_CHUNK), 0)
    done, steps, now = {}, [], 0.0
    while left or tasks or waiting:
        for lane in lanes:
            busy[lane] = [e for e in busy[lane] if e > now]
        pick = None
        for k in left:
            lane = units[k][:2]
            if len(busy[lane]) < 3 and all(arrived.get(p, 1e9) <= now for p in units[k][4]):
                pick = k
                break
        if pick is not None:
            lane = units[pick][:2]
            free[lane] = max(free[lane], now) + length[pick]
            busy[lane].append(free[lane])
            arrived[pick] = free[lane] + hop
            left.remove(pick)
            steps.append(("send", pick))
            now += 0.08
            continue
        task = next((t for t in tasks if t[2] is None and t[3] <= now or t[2] in done and done[t[2]] + t[3] <= now), None)
        if task is not None:
            tasks.remove(task)
            steps.append((task[0], task[1]))
            now += task[4]
            done[f"{task[0]}{task[1]}"] = now
            continue
        picked = None
        if "scale1" in done:
            for f in range(N_CHUNK):
                ready = [p for p in waiting if p[0] == f and all(arrived.get(k, 1e9) <= now for k in arrivals[p])]
                remaining = sum(p[0] == f for p in waiting)
                if len(ready) >= GROUP or ready and len(ready) == remaining:
                    ready.sort(key=lambda p: max([arrived[k] for k in arrivals[p]], default=0.0))
                    picked = ready[:GROUP]
                    break
        if picked:
            for p in picked:
                waiting.remove(p)
            f = picked[0][0]
            steps.append(("multiply", (f, tuple(p[1:] for p in picked), count[f] == 0)))
            count[f] += len(picked)
            now += cost
            if not any(p[0] == f for p in waiting):
                done[f"all{f}"] = now
            continue
        now += 0.05
    return units, arrivals, steps, now


def kernel(
    plan, inv, cols_s, count_s, cols_v, feats, memory_v, tiles_h, conv_w, in_w, hid_w, conv_b, in_b, hid_b, out,
    panel, tiles, acc, sums, deg_out, deg_in, scales, cw, iw, hw, held, own,
    s1, r1, s2, r2, s3, r3, message,
    send_sem, recv_sem, dsem_s, dsem_r, load_sem, rs_s, rs_r,
):
    units, arrivals, steps = plan
    index = {k: i for i, k in enumerate(units)}
    slots, tile = tiles_h.shape[0], tiles_h.shape[1]
    block_rows, width = feats.shape
    wide = width // N_CHUNK
    n_col, n_row = NX * NZ, 2 * NY
    col_blocks = n_col * block_rows // tile
    group_rows = n_row * block_rows
    r = lax.axis_index("row")
    c = lax.axis_index("col")
    x, z = lax.div(c, NZ), lax.rem(c, NZ)
    y, core = lax.div(r, 2), lax.rem(r, 2)

    def col_at(dx, dz):
        return lax.rem(x + (dx + NX), NX) * NZ + lax.rem(z + (dz + NZ), NZ)

    def row_at(dy, other):
        return lax.rem(y + (dy + NY), NY) * 2 + (1 - core if other else core)

    half_slots = slots // 2
    loads = [
        pltpu.make_async_copy(tiles_h.at[pl.ds(i * half_slots, half_slots)], tiles.at[pl.ds(i * half_slots, half_slots)], load_sem.at[i])
        for i in range(2)
    ]
    loads += [pltpu.make_async_copy(a, b, load_sem.at[2 + i]) for i, (a, b) in enumerate(((hid_w, hw), (conv_w, cw), (in_w, iw)))]
    for copy in loads:
        copy.start()

    barrier = pltpu.get_barrier_semaphore()

    @pl.loop(1, n_col)
    def _(i):
        pl.semaphore_signal(barrier, inc=1, device_id=(r, lax.rem(c + i, n_col)), device_id_type=MESH)

    for dy, other in ((0, True), (1, False), (-1, False)):
        pl.semaphore_signal(barrier, inc=1, device_id=(row_at(dy, other), c), device_id_type=MESH)
    for f in range(N_CHUNK):
        panel[f, c] = feats[:, f * wide : (f + 1) * wide]
    pl.semaphore_wait(barrier, n_col - 1 + 3)

    def arrival(key):
        f, _, dx, dz, _ = key
        _, _, lo, hi, _ = units[key]
        spot = panel.at[f, col_at(dx, dz), pl.ds(lo, hi - lo)]
        i = index[key]
        return pltpu.make_async_remote_copy(
            spot, spot, send_sem.at[i], recv_sem.at[i], device_id=(r, c), device_id_type=MESH
        )

    def sending(key):
        f, _, dx, dz, _ = key
        axis, sign, lo, hi, _ = units[key]
        sx, sz = (sign, 0) if axis == "x" else (0, sign)
        spot = panel.at[f, col_at(dx - sx, dz - sz), pl.ds(lo, hi - lo)]
        i = index[key]
        return pltpu.make_async_remote_copy(
            spot, spot, send_sem.at[i], recv_sem.at[i], device_id=(r, col_at(-sx, -sz)), device_id_type=MESH
        )

    waited = set()

    def wait_for(keys):
        for k in keys:
            if k not in waited:
                waited.add(k)
                arrival(k).wait_recv()

    def column_sums(part):
        loads[part].wait()

        @pl.loop(0, half_slots // 8)
        def _(g):
            t0 = pl.multiple_of(part * half_slots + g * 8, 8)
            rows = [jnp.sum(tiles[t0 + k].astype(F32), axis=0, keepdims=True) for k in range(8)]
            sums[pl.ds(t0, 8), :] = jnp.concatenate(rows, axis=0)

    def degree_send(i, first):
        peer = lax.rem(c + i, n_col)
        if first:
            src, dst = deg_out.at[pl.ds(2 * peer, 2)], deg_in.at[c]
        else:
            src = dst = scales.at[pl.ds(2 * c, 2)]
        k = 0 if first else 1
        return pltpu.make_async_remote_copy(
            src, dst, dsem_s.at[k, i], dsem_r.at[k, i], device_id=(r, peer), device_id_type=MESH
        )

    def degrees(part):
        if part == 0:
            block = lax.broadcasted_iota(jnp.int32, (col_blocks, slots), 0)
            slot = lax.broadcasted_iota(jnp.int32, (col_blocks, slots), 1)
            picker = jnp.where((cols_v[...] == block) & (slot < count_s[0]), 1.0, 0.0).astype(F32)
            terms = jnp.dot(picker, sums[...], precision=lax.Precision.HIGHEST, preferred_element_type=F32)
            for b in range(col_blocks):
                deg_out[b] = terms[b : b + 1, :]
            deg_in[c] = deg_out[pl.ds(2 * c, 2)]

            @pl.loop(1, n_col)
            def _(i):
                degree_send(i, True).start()
        else:

            @pl.loop(1, n_col)
            def _(i):
                degree_send(i, True).wait_recv()

            total = jnp.sum(deg_in[...], axis=0)
            scales[pl.ds(2 * c, 2)] = lax.rsqrt(1.0 + total)

            @pl.loop(1, n_col)
            def _(i):
                degree_send(i, False).start()

    def scale(part):
        if part == 0:

            @pl.loop(1, n_col)
            def _(i):
                degree_send(i, False).wait_recv()

            tiles[slots] = jnp.zeros((tile, tile), BF16)

        @pl.loop(0, half_slots // 4)
        def _(g):
            for k in range(4):
                t = part * half_slots + g * 4 + k
                tiles[t] = (tiles[t].astype(F32) * scales[cols_s[t]]).astype(BF16)

    def multiply(f, places, first):
        m_blocks = 4
        spots = [col_at(*place) for place in places]

        @pl.loop(0, group_rows // (tile * m_blocks))
        def _(m):
            total = None
            for s in spots:
                lhs = []
                for a in range(m_blocks):
                    base = (m * m_blocks + a) * col_blocks + 2 * s
                    lhs.append(jnp.concatenate([tiles[inv[base]], tiles[inv[base + 1]]], axis=1))
                term = jnp.dot(jnp.concatenate(lhs, axis=0), panel[f, s], preferred_element_type=F32)
                total = term if total is None else total + term
            rows = pl.ds(pl.multiple_of(m * (m_blocks * tile), m_blocks * tile), m_blocks * tile)
            if first:
                acc[f, rows] = total
            else:
                acc[f, rows] += total

    half = block_rows // 2

    def owner_rows(rr, part=None):
        start = pl.multiple_of(rr * block_rows, block_rows)
        if part is None:
            return pl.ds(start, block_rows)
        return pl.ds(start + part * half, half)

    def rs_core(f):
        return pltpu.make_async_remote_copy(
            s1.at[f], r1.at[f], rs_s.at[f, 0], rs_r.at[f, 0], device_id=(row_at(0, True), c), device_id_type=MESH
        )

    def rs_first(f, up):
        return pltpu.make_async_remote_copy(
            s2.at[f, up], r2.at[f, up], rs_s.at[f, 1 + up], rs_r.at[f, 1 + up],
            device_id=(row_at(1 - 2 * up, False), c), device_id_type=MESH,
        )

    def rs_second(f, up):
        return pltpu.make_async_remote_copy(
            s3.at[f, up], r3.at[f, up], rs_s.at[f, 3 + up], rs_r.at[f, 3 + up],
            device_id=(row_at(1 - 2 * up, False), c), device_id_type=MESH,
        )

    def reduce(f, stage):
        if stage == 0:
            for q in range(NY):
                s1[f, q] = acc[f, owner_rows(q * 2 + (1 - core))].astype(BF16)
            rs_core(f).start()
        elif stage == 1:
            rs_core(f).wait_recv()

            def pair(dy, part):
                rr = row_at(dy, False)
                q = lax.rem(y + (dy + NY), NY)
                return acc[f, owner_rows(rr, part)] + r1[f, q, part * half : (part + 1) * half].astype(F32)

            for up in (0, 1):
                s2[f, up, 0] = pair(2, up).astype(BF16)
                s2[f, up, 1] = pair(1 - 2 * up, 1 - up).astype(BF16)
                rs_first(f, up).start()
            for up in (0, 1):
                own[f, up] = pair(1 - 2 * up, up)
                own[f, 2 + up] = pair(0, up)
        elif stage == 2:
            for up in (0, 1):
                rs_first(f, up).wait_recv()
                s3[f, up] = (own[f, up] + r2[f, up, 0].astype(F32)).astype(BF16)
                rs_second(f, up).start()
        else:
            for up in (0, 1):
                rs_second(f, up).wait_recv()
            for part in (0, 1):
                own[f, 2 + part] += r3[f, part].astype(F32) + r2[f, 1 - part, 1].astype(F32)

    def held_product():
        loads[2].wait()
        bias = hid_b[...]
        low = memory_v[...].astype(BF16)
        for j in range(3 * width // 256):
            part = slice(j * 256, (j + 1) * 256)
            term = jnp.dot(low, hw[:, part], preferred_element_type=F32) + bias[:, part]
            held[:, part] = term

    run = {
        "sums": column_sums,
        "degrees": degrees,
        "scale": scale,
        "held": lambda _: held_product(),
        "reduce": lambda k: reduce(k // 4, k % 4),
    }
    for what, arg in steps:
        if what == "send":
            wait_for(units[arg][4])
            sending(arg).start()
        elif what == "multiply":
            f, places, first = arg
            for place in places:
                wait_for(arrivals[(f, *place)])
            multiply(f, places, first)
        else:
            run[what](arg)

    loads[3].wait()
    loads[4].wait()
    for part in (0, 1):
        rows = slice(part * half, (part + 1) * half)
        owned = [own[f, 2 + part] for f in range(N_CHUNK)]
        square = sum(jnp.sum(o * o, axis=1, keepdims=True) for o in owned) * (1.0 / width)
        root = jnp.sqrt(square + norm_epsilon)
        normed = jnp.concatenate([(o / root).astype(BF16) for o in owned], axis=1)
        value = jnp.dot(normed, cw[...], preferred_element_type=F32) + conv_b[...]
        message[rows] = jnp.maximum(value, 0.0).astype(BF16)
    bias = in_b[...]
    told = message[...]
    for j in range(width // 128):
        low, mid, high = (slice(k * width + j * 128, k * width + (j + 1) * 128) for k in range(3))
        gates = [jnp.dot(told, iw[:, p], preferred_element_type=F32) + bias[:, p] for p in (low, mid, high)]
        reset = jax.nn.sigmoid(gates[0] + held[:, low])
        update = jax.nn.sigmoid(gates[1] + held[:, mid])
        candidate = jnp.tanh(gates[2] + reset * held[:, high])
        out[:, low] = (1.0 - update) * candidate + update * memory_v[:, low]

    for k in units:
        sending(k).wait_send()

    @pl.loop(1, n_col)
    def _(i):
        degree_send(i, True).wait_send()
        degree_send(i, False).wait_send()

    for f in range(N_CHUNK):
        rs_core(f).wait_send()
        for up in (0, 1):
            rs_first(f, up).wait_send()
            rs_second(f, up).wait_send()


def on_device(
    features, memory, tile_values, tile_rows, tile_cols, tile_count,
    conv_weight, conv_bias, input_weight, input_bias, hidden_weight, hidden_bias,
):
    own_rows, width = features.shape
    tiles = tile_values[0, 0]
    slots, tile = tiles.shape[0], tiles.shape[1]
    rows, cols, count = tile_rows[0, 0], tile_cols[0, 0], tile_count[0, 0]
    n_col, n_row = lax.axis_size("col"), lax.axis_size("row")
    row_blocks, col_blocks = own_rows * n_row // tile, own_rows * n_col // tile
    key = jnp.where(jnp.arange(slots) < count, rows * col_blocks + cols, -1)
    spot = jnp.arange(row_blocks * col_blocks)
    hit = key[None, :] == spot[:, None]
    inv = slots + jnp.sum(jnp.where(hit, jnp.arange(slots)[None, :] - slots, 0), axis=1)
    units, arrivals, steps, _ = make_plan(own_rows, width)
    wide = width // N_CHUNK
    half = own_rows // 2
    n = len(units)
    smem = pl.BlockSpec(memory_space=pltpu.SMEM)
    vmem = pl.BlockSpec(memory_space=pltpu.VMEM)
    hbm = pl.BlockSpec(memory_space=pl.ANY)
    return pl.pallas_call(
        functools.partial(kernel, (units, arrivals, steps)),
        out_shape=jax.ShapeDtypeStruct((own_rows, width), F32),
        in_specs=[smem, smem, smem, vmem, vmem, vmem, hbm, hbm, hbm, hbm, vmem, vmem, vmem],
        out_specs=vmem,
        scratch_shapes=[
            pltpu.VMEM((N_CHUNK, n_col, own_rows, wide), BF16),
            pltpu.VMEM((slots + 1, tile, tile), BF16),
            pltpu.VMEM((N_CHUNK, n_row * own_rows, wide), F32),
            pltpu.VMEM((slots, tile), F32),
            pltpu.VMEM((col_blocks, 1, tile), F32),
            pltpu.VMEM((n_col, 2, 1, tile), F32),
            pltpu.VMEM((col_blocks, 1, tile), F32),
            pltpu.VMEM((width, width), BF16),
            pltpu.VMEM((width, 3 * width), BF16),
            pltpu.VMEM((width, 3 * width), BF16),
            pltpu.VMEM((own_rows, 3 * width), F32),
            pltpu.VMEM((N_CHUNK, 4, half, wide), F32),
            pltpu.VMEM((N_CHUNK, NY, own_rows, wide), BF16),
            pltpu.VMEM((N_CHUNK, NY, own_rows, wide), BF16),
            pltpu.VMEM((N_CHUNK, 2, 2, half, wide), BF16),
            pltpu.VMEM((N_CHUNK, 2, 2, half, wide), BF16),
            pltpu.VMEM((N_CHUNK, 2, half, wide), BF16),
            pltpu.VMEM((N_CHUNK, 2, half, wide), BF16),
            pltpu.VMEM((own_rows, width), BF16),
            pltpu.SemaphoreType.DMA((n,)),
            pltpu.SemaphoreType.DMA((n,)),
            pltpu.SemaphoreType.DMA((2, n_col)),
            pltpu.SemaphoreType.DMA((2, n_col)),
            pltpu.SemaphoreType.DMA((5,)),
            pltpu.SemaphoreType.DMA((N_CHUNK, 5)),
            pltpu.SemaphoreType.DMA((N_CHUNK, 5)),
        ],
        compiler_params=pltpu.CompilerParams(
            collective_id=0, has_side_effects=True, vmem_limit_bytes=48 << 20
        ),
    )(
        inv, cols, count.reshape(1), cols.reshape(1, slots), features, memory, tiles,
        conv_weight, input_weight, hidden_weight,
        conv_bias.reshape(1, -1), input_bias.reshape(1, -1), hidden_bias.reshape(1, -1),
    )


def solution(mesh):
    placed = (
        P(("row", "col"), None),
        P(("col", "row"), None),
        P("row", "col", None, None, None),
        P("row", "col", None),
        P("row", "col", None),
        P("row", "col"),
        P(),
        P(),
        P(),
        P(),
        P(),
        P(),
    )
    return jax.shard_map(
        on_device, mesh=mesh, in_specs=placed, out_specs=P(("col", "row"), None), check_vma=False
    )
```

time: 345 us -> 104 us (0.30)
  the two profiles are of different devices: /device:TPU:2 before, /device:TPU:1 now
where the time goes in v1:
time: 104 us
  Pallas kernels  92.8 us (89%)
  local copies, waits for them, and re-layouts  9.38 us (9%)
    pallas_call x1, Pallas kernels, on_device(): pl.pallas_call(functools.partial(kernel, (units, arrivals, steps)), out_s...  92.8 us
    unnamed x15, local copies, waits for them, and re-layouts  7.98 us

profile of v1, /device:TPU:1, one launch (start us, length us, event | category | flops | bytes accessed | tf_op | source)
XLA Modules:
  0.0 103.7 jit_solution(2394019639258703180)
XLA Ops:
  0.7 0.7 compare_select_fusion
  1.3 0.2 select_reduce_fusion
  1.6 0.7 reshape.32.in_b
  2.3 0.7 reshape.33.hid_b
  3.0 0.0 copy-start
  3.0 1.4 %copy-done = bf16[512,1536]{1,0:T(8,128)(2,1)S(1)} copy-done((bf16[512,1536]{1,0:T(8,128)(2,1)S(1)}, bf16[512,1536]{1,0:T(8,128)(2,1)}, u32[]{:S(2)}) %copy-start) | copy-done | bytes 1572888
  4.4 0.0 copy-start.1
  4.4 1.4 %copy-done.1 = bf16[512,1536]{1,0:T(8,128)(2,1)S(1)} copy-done((bf16[512,1536]{1,0:T(8,128)(2,1)S(1)}, bf16[512,1536]{1,0:T(8,128)(2,1)}, u32[]{:S(2)}) %copy-start.1) | copy-done | bytes 1572888
  5.8 0.0 copy-start.2
  5.8 1.0 %copy-done.2 = f32[256,512]{1,0:T(8,128)S(1)} copy-done((f32[256,512]{1,0:T(8,128)S(1)}, f32[256,512]{1,0:T(8,128)}, u32[]{:S(2)}) %copy-start.2) | copy-done | bytes 524312
  6.8 0.0 copy-start.3
  6.8 1.0 %copy-done.3 = bf16[512,512]{1,0:T(8,128)(2,1)S(1)} copy-done((bf16[512,512]{1,0:T(8,128)(2,1)S(1)}, bf16[512,512]{1,0:T(8,128)(2,1)}, u32[]{:S(2)}) %copy-start.3) | copy-done | bytes 524312
  7.9 0.0 copy-start.4
  7.9 0.9 copy-done.4
  8.8 0.0 copy-start.5
  8.8 0.7 copy-done.5
  9.5 0.0 copy-start.6
  9.5 0.7 copy-done.6
  10.2 92.8 %shard_map.118 = f32[256,512]{1,0:T(8,128)S(1)} custom-call(s32[1024]{0:T(1024)S(1)} %broadcast_add_fusion.inv, s32[128]{0:T(128)S(1)} %bitcast.13, s32[1]{0:T(128)} %bitcast.12.count_s, s32[1,128]{1,0:T(1,128)S(1)} %bitcast.14, bf16[256,512]{1,0:T(8,128)(2,1)S(1)} %copy-done.4, f32[256,512]{1,0:T(8,128)S(1)} %copy-done.2, bf16[128,128,128]{2,1,0:T(8,128)(2,1)} %bitcast.16, ...), custom_call_target="tpu_custom_call" | custom-call | tf_op jit(solution)/shard_map/pallas_call | solution.py:439
  102.9 0.8 copy.15
  (1 shorter events, 0.0 us)
Async XLA Ops:
  3.0 1.4 %copy-start = (bf16[512,1536]{1,0:T(8,128)(2,1)S(1)}, bf16[512,1536]{1,0:T(8,128)(2,1)}, u32[]{:S(2)}) copy-start(bf16[512,1536]{1,0:T(8,128)(2,1)} %in_w.1) | copy-start | bytes 4718596
  4.4 1.4 %copy-start.1 = (bf16[512,1536]{1,0:T(8,128)(2,1)S(1)}, bf16[512,1536]{1,0:T(8,128)(2,1)}, u32[]{:S(2)}) copy-start(bf16[512,1536]{1,0:T(8,128)(2,1)} %hid_w.1) | copy-start | bytes 4718596
  5.8 1.0 %copy-start.2 = (f32[256,512]{1,0:T(8,128)S(1)}, f32[256,512]{1,0:T(8,128)}, u32[]{:S(2)}) copy-start(f32[256,512]{1,0:T(8,128)} %memory_v.1) | copy-start | bytes 1572868
  6.8 1.0 %copy-start.3 = (bf16[512,512]{1,0:T(8,128)(2,1)S(1)}, bf16[512,512]{1,0:T(8,128)(2,1)}, u32[]{:S(2)}) copy-start(bf16[512,512]{1,0:T(8,128)(2,1)} %conv_w.1) | copy-start | bytes 1572868
  7.9 0.9 copy-start.4
  8.8 0.7 copy-start.5
  9.5 0.7 copy-start.6

commit v2 on v1

--- a/solution.py
+++ b/solution.py
@@ -10,9 +10,9 @@
 norm_epsilon = 1e-06
 NX, NZ = 4, 8
 NY = 4
-ROWS_A = 96
+ROWS_A = (96, 96)
 N_CHUNK = 2
-GROUP = 2
+GROUP = 4
 MESH = pl.DeviceIdType.MESH
 F32 = jnp.float32
 BF16 = jnp.bfloat16
@@ -50,13 +50,13 @@
 def make_plan(block_rows, width):
     units, arrivals = {}, {}
     for f in range(N_CHUNK):
-        for part, rows in ((0, (0, ROWS_A)), (1, (ROWS_A, block_rows))):
+        for part, rows in ((0, (0, ROWS_A[f])), (1, (ROWS_A[f], block_rows))):
             more, at = block_units(f, part, rows)
             units.update(more)
             for place, keys in at.items():
                 arrivals.setdefault((f, *place), []).extend(keys)
     per_row = width // N_CHUNK * 2 * 2 / 90e3
-    hop = 0.9
+    hop = 1.5
     length = {k: (u[3] - u[2]) * per_row for k, u in units.items()}
     after = {k: [] for k in units}
     for k, u in units.items():
@@ -73,7 +73,7 @@
     lanes = [(a, s) for a in "xz" for s in (1, -1)]
     arrived, free, busy = {}, dict.fromkeys(lanes, 0.0), {lane: [] for lane in lanes}
     left = list(order)
-    cost = 16.5 / (N_CHUNK * 16) * GROUP / 2
+    cost = 22.0 / (N_CHUNK * 32) * GROUP
     tasks = [
         ["sums", 0, None, 2.0, 1.0],
         ["sums", 1, "sums0", 0.0, 1.0],
@@ -84,10 +84,12 @@
     ]
     for f in range(N_CHUNK):
         tasks += [
-            ["reduce", 4 * f, f"all{f}", 0.0, 0.5],
-            ["reduce", 4 * f + 1, f"reduce{4 * f}", 3.5, 0.5],
-            ["reduce", 4 * f + 2, f"reduce{4 * f + 1}", 5.0, 0.3],
-            ["reduce", 4 * f + 3, f"reduce{4 * f + 2}", 5.0, 0.3],
+            ["reduce", 6 * f, f"all{f}", 0.0, 0.5],
+            ["reduce", 6 * f + 1, f"reduce{6 * f}", 2.0, 0.2],
+            ["reduce", 6 * f + 2, f"reduce{6 * f + 1}", 0.0, 0.3],
+            ["reduce", 6 * f + 3, f"reduce{6 * f + 2}", 0.0, 0.3],
+            ["reduce", 6 * f + 4, f"reduce{6 * f + 3}", 3.0, 0.3],
+            ["reduce", 6 * f + 5, f"reduce{6 * f + 4}", 4.0, 0.3],
         ]
     tasks.append(["held", 0, "scale1", 0.0, 2.0])
     sources = [p for p in arrivals if p not in [(f, 0, 0) for f in range(N_CHUNK)]]
@@ -100,7 +102,7 @@
         pick = None
         for k in left:
             lane = units[k][:2]
-            if len(busy[lane]) < 3 and all(arrived.get(p, 1e9) <= now for p in units[k][4]):
+            if len(busy[lane]) < 5 and all(arrived.get(p, 1e9) <= now for p in units[k][4]):
                 pick = k
                 break
         if pick is not None:
@@ -143,19 +145,20 @@
 
 
 def kernel(
-    plan, inv, cols_s, count_s, cols_v, feats, memory_v, tiles_h, conv_w, in_w, hid_w, conv_b, in_b, hid_b, out,
+    plan, inv, cols_s, count_s, feats_h, memory_h, tiles_h, cols_h, conv_w, conv_b, in_w, in_b, hid_w, hid_b, out,
     panel, tiles, acc, sums, deg_out, deg_in, scales, cw, iw, hw, held, own,
-    s1, r1, s2, r2, s3, r3, message,
+    s1, r1, s2, r2, s3, r3, message, memory_v, cols_v, cb, ib, hb,
     send_sem, recv_sem, dsem_s, dsem_r, load_sem, rs_s, rs_r,
 ):
     units, arrivals, steps = plan
     index = {k: i for i, k in enumerate(units)}
-    slots, tile = tiles_h.shape[0], tiles_h.shape[1]
-    block_rows, width = feats.shape
+    slots, tile = tiles_h.shape[2], tiles_h.shape[3]
+    block_rows, width = feats_h.shape
     wide = width // N_CHUNK
     n_col, n_row = NX * NZ, 2 * NY
     col_blocks = n_col * block_rows // tile
     group_rows = n_row * block_rows
+    row_blocks = group_rows // tile
     r = lax.axis_index("row")
     c = lax.axis_index("col")
     x, z = lax.div(c, NZ), lax.rem(c, NZ)
@@ -168,12 +171,15 @@
         return lax.rem(y + (dy + NY), NY) * 2 + (1 - core if other else core)
 
     half_slots = slots // 2
-    loads = [
-        pltpu.make_async_copy(tiles_h.at[pl.ds(i * half_slots, half_slots)], tiles.at[pl.ds(i * half_slots, half_slots)], load_sem.at[i])
-        for i in range(2)
-    ]
-    loads += [pltpu.make_async_copy(a, b, load_sem.at[2 + i]) for i, (a, b) in enumerate(((hid_w, hw), (conv_w, cw), (in_w, iw)))]
-    for copy in loads:
+    moves = {f"own{f}": (feats_h.at[:, pl.ds(f * wide, wide)], panel.at[f, c]) for f in range(N_CHUNK)}
+    moves["cols"] = (cols_h, cols_v)
+    for i in range(2):
+        part = pl.ds(i * half_slots, half_slots)
+        moves[f"tiles{i}"] = (tiles_h.at[0, 0, part], tiles.at[part])
+    moves |= {"memory": (memory_h, memory_v), "hid_w": (hid_w, hw), "hid_b": (hid_b, hb)}
+    moves |= {"conv_w": (conv_w, cw), "conv_b": (conv_b, cb), "in_w": (in_w, iw), "in_b": (in_b, ib)}
+    loads = {k: pltpu.make_async_copy(*ends, load_sem.at[i]) for i, (k, ends) in enumerate(moves.items())}
+    for copy in loads.values():
         copy.start()
 
     barrier = pltpu.get_barrier_semaphore()
@@ -185,7 +191,7 @@
     for dy, other in ((0, True), (1, False), (-1, False)):
         pl.semaphore_signal(barrier, inc=1, device_id=(row_at(dy, other), c), device_id_type=MESH)
     for f in range(N_CHUNK):
-        panel[f, c] = feats[:, f * wide : (f + 1) * wide]
+        loads[f"own{f}"].wait()
     pl.semaphore_wait(barrier, n_col - 1 + 3)
 
     def arrival(key):
@@ -216,7 +222,7 @@
                 arrival(k).wait_recv()
 
     def column_sums(part):
-        loads[part].wait()
+        loads[f"tiles{part}"].wait()
 
         @pl.loop(0, half_slots // 8)
         def _(g):
@@ -237,9 +243,10 @@
 
     def degrees(part):
         if part == 0:
+            loads["cols"].wait()
             block = lax.broadcasted_iota(jnp.int32, (col_blocks, slots), 0)
             slot = lax.broadcasted_iota(jnp.int32, (col_blocks, slots), 1)
-            picker = jnp.where((cols_v[...] == block) & (slot < count_s[0]), 1.0, 0.0).astype(F32)
+            picker = jnp.where((cols_v[0] == block) & (slot < count_s[0, 0]), 1.0, 0.0).astype(F32)
             terms = jnp.dot(picker, sums[...], precision=lax.Precision.HIGHEST, preferred_element_type=F32)
             for b in range(col_blocks):
                 deg_out[b] = terms[b : b + 1, :]
@@ -274,27 +281,25 @@
         def _(g):
             for k in range(4):
                 t = part * half_slots + g * 4 + k
-                tiles[t] = (tiles[t].astype(F32) * scales[cols_s[t]]).astype(BF16)
+                tiles[t] = (tiles[t].astype(F32) * scales[cols_s[0, 0, t]]).astype(BF16)
 
     def multiply(f, places, first):
-        m_blocks = 4
+        m_blocks = row_blocks // 2
         spots = [col_at(*place) for place in places]
 
-        @pl.loop(0, group_rows // (tile * m_blocks))
+        @pl.loop(0, row_blocks // m_blocks)
         def _(m):
-            total = None
-            for s in spots:
-                lhs = []
-                for a in range(m_blocks):
-                    base = (m * m_blocks + a) * col_blocks + 2 * s
-                    lhs.append(jnp.concatenate([tiles[inv[base]], tiles[inv[base + 1]]], axis=1))
-                term = jnp.dot(jnp.concatenate(lhs, axis=0), panel[f, s], preferred_element_type=F32)
-                total = term if total is None else total + term
+            lhs = []
+            for a in range(m_blocks):
+                blocks = [tiles[inv[(m * m_blocks + a) * col_blocks + (2 * s + k)]] for s in spots for k in range(2)]
+                lhs.append(jnp.concatenate(blocks, axis=1))
+            rhs = jnp.concatenate([panel[f, s] for s in spots], axis=0)
+            term = jnp.dot(jnp.concatenate(lhs, axis=0), rhs, preferred_element_type=F32)
             rows = pl.ds(pl.multiple_of(m * (m_blocks * tile), m_blocks * tile), m_blocks * tile)
             if first:
-                acc[f, rows] = total
+                acc[f, rows] = term
             else:
-                acc[f, rows] += total
+                acc[f, rows] += term
 
     half = block_rows // 2
 
@@ -304,57 +309,67 @@
             return pl.ds(start, block_rows)
         return pl.ds(start + part * half, half)
 
-    def rs_core(f):
+    order = (2, 1, -1, 0)
+
+    def rs_core(f, k):
         return pltpu.make_async_remote_copy(
-            s1.at[f], r1.at[f], rs_s.at[f, 0], rs_r.at[f, 0], device_id=(row_at(0, True), c), device_id_type=MESH
+            s1.at[f, k], r1.at[f, k], rs_s.at[f, k], rs_r.at[f, k], device_id=(row_at(0, True), c), device_id_type=MESH
         )
 
-    def rs_first(f, up):
+    def rs_first(f, up, k):
+        i = 4 + 2 * up + k
         return pltpu.make_async_remote_copy(
-            s2.at[f, up], r2.at[f, up], rs_s.at[f, 1 + up], rs_r.at[f, 1 + up],
+            s2.at[f, up, k], r2.at[f, up, k], rs_s.at[f, i], rs_r.at[f, i],
             device_id=(row_at(1 - 2 * up, False), c), device_id_type=MESH,
         )
 
     def rs_second(f, up):
         return pltpu.make_async_remote_copy(
-            s3.at[f, up], r3.at[f, up], rs_s.at[f, 3 + up], rs_r.at[f, 3 + up],
+            s3.at[f, up], r3.at[f, up], rs_s.at[f, 8 + up], rs_r.at[f, 8 + up],
             device_id=(row_at(1 - 2 * up, False), c), device_id_type=MESH,
         )
 
+    def pair(f, dy, part):
+        k = order.index(dy)
+        return acc[f, owner_rows(row_at(dy, False), part)] + r1[f, k, part * half : (part + 1) * half].astype(F32)
+
     def reduce(f, stage):
         if stage == 0:
-            for q in range(NY):
-                s1[f, q] = acc[f, owner_rows(q * 2 + (1 - core))].astype(BF16)
-            rs_core(f).start()
+            for k, dy in enumerate(order):
+                s1[f, k] = acc[f, owner_rows(row_at(dy, True))].astype(BF16)
+                rs_core(f, k).start()
         elif stage == 1:
-            rs_core(f).wait_recv()
-
-            def pair(dy, part):
-                rr = row_at(dy, False)
-                q = lax.rem(y + (dy + NY), NY)
-                return acc[f, owner_rows(rr, part)] + r1[f, q, part * half : (part + 1) * half].astype(F32)
-
+            rs_core(f, 0).wait_recv()
             for up in (0, 1):
-                s2[f, up, 0] = pair(2, up).astype(BF16)
-                s2[f, up, 1] = pair(1 - 2 * up, 1 - up).astype(BF16)
-                rs_first(f, up).start()
-            for up in (0, 1):
-                own[f, up] = pair(1 - 2 * up, up)
-                own[f, 2 + up] = pair(0, up)
+                s2[f, up, 0] = pair(f, 2, up).astype(BF16)
+                rs_first(f, up, 0).start()
         elif stage == 2:
             for up in (0, 1):
-                rs_first(f, up).wait_recv()
+                rs_core(f, 1 + up).wait_recv()
+                s2[f, up, 1] = pair(f, 1 - 2 * up, 1 - up).astype(BF16)
+                rs_first(f, up, 1).start()
+        elif stage == 3:
+            rs_core(f, 3).wait_recv()
+            for up in (0, 1):
+                own[f, up] = pair(f, 1 - 2 * up, up)
+                own[f, 2 + up] = pair(f, 0, up)
+        elif stage == 4:
+            for up in (0, 1):
+                rs_first(f, up, 0).wait_recv()
                 s3[f, up] = (own[f, up] + r2[f, up, 0].astype(F32)).astype(BF16)
                 rs_second(f, up).start()
         else:
             for up in (0, 1):
+                rs_first(f, up, 1).wait_recv()
+                own[f, 3 - up] += r2[f, up, 1].astype(F32)
+            for up in (0, 1):
                 rs_second(f, up).wait_recv()
-            for part in (0, 1):
-                own[f, 2 + part] += r3[f, part].astype(F32) + r2[f, 1 - part, 1].astype(F32)
+                own[f, 2 + up] += r3[f, up].astype(F32)
 
     def held_product():
-        loads[2].wait()
-        bias = hid_b[...]
+        for name in ("memory", "hid_w", "hid_b"):
+            loads[name].wait()
+        bias = hb[...].reshape(1, -1)
         low = memory_v[...].astype(BF16)
         for j in range(3 * width // 256):
             part = slice(j * 256, (j + 1) * 256)
@@ -366,7 +381,7 @@
         "degrees": degrees,
         "scale": scale,
         "held": lambda _: held_product(),
-        "reduce": lambda k: reduce(k // 4, k % 4),
+        "reduce": lambda k: reduce(k // 6, k % 6),
     }
     for what, arg in steps:
         if what == "send":
@@ -380,20 +395,20 @@
         else:
             run[what](arg)
 
-    loads[3].wait()
-    loads[4].wait()
+    for name in ("conv_w", "conv_b", "in_w", "in_b"):
+        loads[name].wait()
     for part in (0, 1):
         rows = slice(part * half, (part + 1) * half)
         owned = [own[f, 2 + part] for f in range(N_CHUNK)]
         square = sum(jnp.sum(o * o, axis=1, keepdims=True) for o in owned) * (1.0 / width)
         root = jnp.sqrt(square + norm_epsilon)
         normed = jnp.concatenate([(o / root).astype(BF16) for o in owned], axis=1)
-        value = jnp.dot(normed, cw[...], preferred_element_type=F32) + conv_b[...]
+        value = jnp.dot(normed, cw[...], preferred_element_type=F32) + cb[...].reshape(1, -1)
         message[rows] = jnp.maximum(value, 0.0).astype(BF16)
-    bias = in_b[...]
+    bias = ib[...].reshape(1, -1)
     told = message[...]
-    for j in range(width // 128):
-        low, mid, high = (slice(k * width + j * 128, k * width + (j + 1) * 128) for k in range(3))
+    for j in range(width // 256):
+        low, mid, high = (slice(k * width + j * 256, k * width + (j + 1) * 256) for k in range(3))
         gates = [jnp.dot(told, iw[:, p], preferred_element_type=F32) + bias[:, p] for p in (low, mid, high)]
         reset = jax.nn.sigmoid(gates[0] + held[:, low])
         update = jax.nn.sigmoid(gates[1] + held[:, mid])
@@ -409,9 +424,11 @@
         degree_send(i, False).wait_send()
 
     for f in range(N_CHUNK):
-        rs_core(f).wait_send()
+        for k in range(NY):
+            rs_core(f, k).wait_send()
         for up in (0, 1):
-            rs_first(f, up).wait_send()
+            rs_first(f, up, 0).wait_send()
+            rs_first(f, up, 1).wait_send()
             rs_second(f, up).wait_send()
 
 
@@ -420,26 +437,24 @@
     conv_weight, conv_bias, input_weight, input_bias, hidden_weight, hidden_bias,
 ):
     own_rows, width = features.shape
-    tiles = tile_values[0, 0]
-    slots, tile = tiles.shape[0], tiles.shape[1]
-    rows, cols, count = tile_rows[0, 0], tile_cols[0, 0], tile_count[0, 0]
+    slots, tile = tile_values.shape[2], tile_values.shape[3]
     n_col, n_row = lax.axis_size("col"), lax.axis_size("row")
     row_blocks, col_blocks = own_rows * n_row // tile, own_rows * n_col // tile
-    key = jnp.where(jnp.arange(slots) < count, rows * col_blocks + cols, -1)
-    spot = jnp.arange(row_blocks * col_blocks)
-    hit = key[None, :] == spot[:, None]
-    inv = slots + jnp.sum(jnp.where(hit, jnp.arange(slots)[None, :] - slots, 0), axis=1)
+    slot = jnp.arange(slots)
+    key = jnp.where(slot < tile_count[0, 0], tile_rows[0, 0] * col_blocks + tile_cols[0, 0], -1)
+    hit = key[None, :] == jnp.arange(row_blocks * col_blocks)[:, None]
+    inv = slots + jnp.sum(jnp.where(hit, slot[None, :] - slots, 0), axis=1)
     units, arrivals, steps, _ = make_plan(own_rows, width)
     wide = width // N_CHUNK
     half = own_rows // 2
     n = len(units)
     smem = pl.BlockSpec(memory_space=pltpu.SMEM)
     vmem = pl.BlockSpec(memory_space=pltpu.VMEM)
-    hbm = pl.BlockSpec(memory_space=pl.ANY)
+    hbm = pl.BlockSpec(memory_space=pltpu.HBM)
     return pl.pallas_call(
         functools.partial(kernel, (units, arrivals, steps)),
         out_shape=jax.ShapeDtypeStruct((own_rows, width), F32),
-        in_specs=[smem, smem, smem, vmem, vmem, vmem, hbm, hbm, hbm, hbm, vmem, vmem, vmem],
+        in_specs=[smem] * 3 + [hbm] * 10,
         out_specs=vmem,
         scratch_shapes=[
             pltpu.VMEM((N_CHUNK, n_col, own_rows, wide), BF16),
@@ -461,21 +476,31 @@
             pltpu.VMEM((N_CHUNK, 2, half, wide), BF16),
             pltpu.VMEM((N_CHUNK, 2, half, wide), BF16),
             pltpu.VMEM((own_rows, width), BF16),
+            pltpu.VMEM((own_rows, width), F32),
+            pltpu.VMEM((1, 1, slots), jnp.int32),
+            pltpu.VMEM((width,), F32),
+            pltpu.VMEM((3 * width,), F32),
+            pltpu.VMEM((3 * width,), F32),
             pltpu.SemaphoreType.DMA((n,)),
             pltpu.SemaphoreType.DMA((n,)),
             pltpu.SemaphoreType.DMA((2, n_col)),
             pltpu.SemaphoreType.DMA((2, n_col)),
-            pltpu.SemaphoreType.DMA((5,)),
-            pltpu.SemaphoreType.DMA((N_CHUNK, 5)),
-            pltpu.SemaphoreType.DMA((N_CHUNK, 5)),
+            pltpu.SemaphoreType.DMA((20,)),
+            pltpu.SemaphoreType.DMA((N_CHUNK, 10)),
+            pltpu.SemaphoreType.DMA((N_CHUNK, 10)),
         ],
         compiler_params=pltpu.CompilerParams(
             collective_id=0, has_side_effects=True, vmem_limit_bytes=48 << 20
         ),
     )(
-        inv, cols, count.reshape(1), cols.reshape(1, slots), features, memory, tiles,
-        conv_weight, input_weight, hidden_weight,
-        conv_bias.reshape(1, -1), input_bias.reshape(1, -1), hidden_bias.reshape(1, -1),
+        inv, tile_cols, tile_count,
+        *[
+            pltpu.with_memory_space_constraint(a, pltpu.HBM)
+            for a in (
+                features, memory, tile_values, tile_cols,
+                conv_weight, conv_bias, input_weight, input_bias, hidden_weight, hidden_bias,
+            )
+        ],
     )
 
 

time: 104 us -> 82.4 us (0.79)
  the two profiles are of different devices: /device:TPU:1 before, /device:TPU:2 now
where the time goes in v2:
time: 82.4 us; the launch traced here: 82.3 us
  Pallas kernels  79.9 us (97%)
  other arithmetic  0.89 us (1%)
    pallas_call x1, Pallas kernels, on_device(): pl.pallas_call(functools.partial(kernel, (units, arrivals, steps)), out_s...  79.9 us

profile of v2, /device:TPU:2, one launch (start us, length us, event | category | flops | bytes accessed | tf_op | source)
XLA Modules:
  0.0 82.3 jit_solution(17291916458129596383)
XLA Ops:
  0.7 0.7 compare_select_fusion
  1.3 0.2 select_reduce_fusion
  1.6 79.9 %shard_map.118 = f32[256,512]{1,0:T(8,128)S(1)} custom-call(s32[1024]{0:T(1024)S(1)} %broadcast_add_fusion.inv, s32[1,1,128]{2,1,0:T(1,128)} %cols_h.1, s32[1,1]{1,0:T(1,128)} %copy.14.count_s, bf16[256,512]{1,0:T(8,128)(2,1)} %feats_h.1, f32[256,512]{1,0:T(8,128)} %memory_h.1, bf16[1,1,128,128,128]{4,3,2,1,0:T(8,128)(2,1)} %tiles_h.1, s32[1,1,128]{2,1,0:T(1,128)} %cols_h.1, ...), custom_call_target="tpu_custom_call" | custom-call | tf_op jit(solution)/shard_map/pallas_call | solution.py:454
  81.5 0.8 copy.15
  (1 shorter events, 0.0 us)

commit v3 on v2

--- a/solution.py
+++ b/solution.py
@@ -56,7 +56,7 @@
             for place, keys in at.items():
                 arrivals.setdefault((f, *place), []).extend(keys)
     per_row = width // N_CHUNK * 2 * 2 / 90e3
-    hop = 1.5
+    hop = 0.6
     length = {k: (u[3] - u[2]) * per_row for k, u in units.items()}
     after = {k: [] for k in units}
     for k, u in units.items():
@@ -376,6 +376,15 @@
             term = jnp.dot(low, hw[:, part], preferred_element_type=F32) + bias[:, part]
             held[:, part] = term
 
+    def sends_left():
+        for k in units:
+            sending(k).wait_send()
+
+        @pl.loop(1, n_col)
+        def _(i):
+            degree_send(i, True).wait_send()
+            degree_send(i, False).wait_send()
+
     run = {
         "sums": column_sums,
         "degrees": degrees,
@@ -393,6 +402,8 @@
                 wait_for(arrivals[(f, *place)])
             multiply(f, places, first)
         else:
+            if what == "reduce" and arg == 6 * N_CHUNK - 2:
+                sends_left()
             run[what](arg)
 
     for name in ("conv_w", "conv_b", "in_w", "in_b"):
@@ -414,14 +425,6 @@
         update = jax.nn.sigmoid(gates[1] + held[:, mid])
         candidate = jnp.tanh(gates[2] + reset * held[:, high])
         out[:, low] = (1.0 - update) * candidate + update * memory_v[:, low]
-
-    for k in units:
-        sending(k).wait_send()
-
-    @pl.loop(1, n_col)
-    def _(i):
-        degree_send(i, True).wait_send()
-        degree_send(i, False).wait_send()
 
     for f in range(N_CHUNK):
         for k in range(NY):

time: 82.4 us -> 81.5 us (0.989); the launches traced: 82.3 us -> 79.9 us
  Pallas kernels: 79.9 us -> 77.5 us
    pallas_call x1, Pallas kernels: 79.9 us -> 77.5 us  [on_device(): pl.pallas_call(functools.partial(kernel, (units, arrivals, steps)), out_s...]
where the time goes in v3:
time: 81.5 us; the launch traced here: 79.9 us
  Pallas kernels  77.5 us (95%)
  other arithmetic  0.89 us (1%)
    pallas_call x1, Pallas kernels, on_device(): pl.pallas_call(functools.partial(kernel, (units, arrivals, steps)), out_s...  77.5 us

profile of v3, /device:TPU:2, one launch (start us, length us, event | category | flops | bytes accessed | tf_op | source)
XLA Modules:
  0.0 79.9 jit_solution(919098054915748792)
XLA Ops:
  0.7 0.7 compare_select_fusion
  1.3 0.2 select_reduce_fusion
  1.6 77.5 %shard_map.118 = f32[256,512]{1,0:T(8,128)S(1)} custom-call(s32[1024]{0:T(1024)S(1)} %broadcast_add_fusion.inv, s32[1,1,128]{2,1,0:T(1,128)} %cols_h.1, s32[1,1]{1,0:T(1,128)} %copy.14.count_s, bf16[256,512]{1,0:T(8,128)(2,1)} %feats_h.1, f32[256,512]{1,0:T(8,128)} %memory_h.1, bf16[1,1,128,128,128]{4,3,2,1,0:T(8,128)(2,1)} %tiles_h.1, s32[1,1,128]{2,1,0:T(1,128)} %cols_h.1, ...), custom_call_target="tpu_custom_call" | custom-call | tf_op jit(solution)/shard_map/pallas_call | solution.py:457
  79.1 0.8 copy.15
  (1 shorter events, 0.0 us)
